TPU v7x, 512 devices: a whole 4x4x16 slice. The times are simulated.
512 devices in a mesh: dp: 4 (over x), cand: 32 (over z, core), tensor: 4 (over y).
Axes of the slice: x: 4, y: 4, z: 16, core: 2. Of those that a mesh axis runs over, the one named last changes fastest.
Arguments:
- context: bfloat16 [8, 4096, 3584], P('dp', 'cand', 'tensor'), may hold values from -12 to 12
- residual: bfloat16 [8, 4096, 3584], P('dp', ('cand', 'tensor')), may hold values from -36 to 36
- out_weight: bfloat16 [3584, 3584], P('cand', 'tensor'), may hold values from -0.09375 to 0.09375
- adapter_down: bfloat16 [3584, 16], P('tensor'), may hold values from -0.09375 to 0.09375
- adapter_up_weight: bfloat16 [16, 3584], replicated, may hold values from -1.5 to 1.5
- norm_gain: float32 [3584], replicated, may hold values from 0.5 to 1.5
- score_weight: float32 [3584], replicated, may hold values from -0.09375 to 0.09375
- teacher: bfloat16 [8, 4096, 4096], P('dp', 'cand', 'tensor'), may hold values from 0.019897461 to 0.9765625
- pair_mask: int32 [8, 4096, 4096], P('dp', 'cand', 'tensor'), may hold values from 0 to 1, as said below
- loss_scale: float32 [8], P('dp'), may hold values from 65536 to 262144
Outputs:
- context_grad: bfloat16 [8, 4096, 3584], P('dp', 'cand', 'tensor')
- residual_gradient: bfloat16 [8, 4096, 3584], P('dp', ('cand', 'tensor'))
- down_grad: float32 [3584, 16], P('tensor')
- up_weight_gradient: float32 [16, 3584], P(None, 'tensor')
- pair_loss: float32 [8], P('dp')
Inputs may be any that keep to these rules, and one draw needn't show every extreme that they name: pair_mask holds 0 or 1; with P = 32, every pair (i, j) whose group j // P lies 4096 / (2P) groups after i // P, counted round over the 4096 / P groups, is valid.
All inputs are finite; a program needn't handle non-finite values.
Results may differ from a plain program's by a relative error of at most 0.02.
Values may be sent and summed in bfloat16 or wider, within the bound.
No kernel may reach another device: no remote copies, remote signals or barrier semaphores. Data moves between devices by JAX's collectives and lax.ppermute only.
A program may use at most 64 MiB of HBM per device.

v0:
```python
import jax
import jax.numpy as jnp
from jax import lax
from jax.sharding import PartitionSpec as P

ADAPTER_SCALE = 0.5
epsilon = 1e-06


def rounded(term):
    return lax.optimization_barrier(term.astype(jnp.bfloat16)).astype(jnp.float32)


def pair_terms(all_scores, own_scores, teacher, valid_pairs, row_start, col_start):
    column_scores = lax.dynamic_slice_in_dim(all_scores, col_start, teacher.shape[2], 1)
    margin = own_scores[:, :, None] - column_scores[:, None, :]
    target = teacher.astype(jnp.float32)
    total = jnp.sum(valid_pairs * (jax.nn.softplus(margin) - target * margin), axis=(1, 2))
    slope = valid_pairs * (jax.nn.sigmoid(margin) - target)
    blank = jnp.zeros(all_scores.shape, jnp.float32)
    row_part = lax.dynamic_update_slice_in_dim(blank, jnp.sum(slope, axis=2), row_start, 1)
    column_part = lax.dynamic_update_slice_in_dim(blank, jnp.sum(slope, axis=1), col_start, 1)
    return (total, row_part - column_part)


def on_device(
    context,
    residual,
    out_weight,
    adapter_down,
    adapter_up_weight,
    norm_gain,
    score_weight,
    teacher,
    pair_mask,
    loss_scale,
):
    cand_rows = context.shape[1]
    tensor_count = lax.axis_size("tensor")
    share = cand_rows // tensor_count
    tensor_index = lax.axis_index("tensor")
    group_index = lax.axis_index("cand")
    valid_pairs = pair_mask.astype(jnp.float32)
    mask_count = jnp.sum(valid_pairs, axis=(1, 2))
    count = lax.psum(mask_count, ("cand", "tensor"))
    low_terms = rounded(
        jnp.einsum("qch,hr->qcr", context, adapter_down, preferred_element_type=jnp.float32)
    )
    full_weight = lax.all_gather(out_weight, "cand", axis=0, tiled=True)
    head_terms = jnp.einsum("qch,dh->qcd", context, full_weight, preferred_element_type=jnp.float32)
    head_terms = rounded(head_terms)
    summed_output, low_sum = (
        lax.psum_scatter(
            head_terms.astype(jnp.bfloat16), "tensor", scatter_dimension=1, tiled=True
        ).astype(jnp.float32),
        lax.psum_scatter(
            low_terms.astype(jnp.bfloat16), "tensor", scatter_dimension=1, tiled=True
        ).astype(jnp.float32),
    )
    adapter_input_rows = low_sum.astype(jnp.bfloat16)
    lifted_rows = jnp.einsum(
        "qcr,rd->qcd", adapter_input_rows, adapter_up_weight, preferred_element_type=jnp.float32
    )
    hidden_state = (
        residual.astype(jnp.float32) + summed_output + ADAPTER_SCALE * lifted_rows
    ).astype(jnp.bfloat16)
    hidden_wide = hidden_state.astype(jnp.float32)
    inv_rms = lax.rsqrt(jnp.mean(hidden_wide * hidden_wide, axis=2, keepdims=True) + epsilon)
    scores = jnp.sum(hidden_wide * inv_rms * norm_gain * score_weight, axis=2)
    all_scores = lax.all_gather(scores, ("cand", "tensor"), axis=1, tiled=True)
    own_start = group_index * cand_rows + tensor_index * share
    row_start = group_index * cand_rows
    col_start = tensor_index * teacher.shape[2]
    own_scores = lax.dynamic_slice_in_dim(all_scores, row_start, cand_rows, 1)
    total, score_vector = pair_terms(
        all_scores, own_scores, teacher, valid_pairs, row_start, col_start
    )
    summed_grad, loss_sum = lax.psum((score_vector, total), ("cand", "tensor"))
    pair_loss = loss_sum / count
    factor = loss_scale / count
    score_grad = lax.dynamic_slice_in_dim(summed_grad, own_start, share, 1) * factor[:, None]
    back_step = score_grad[:, :, None] * norm_gain * score_weight
    grad_hidden = inv_rms * back_step - hidden_wide * inv_rms**3 * jnp.mean(
        hidden_wide * back_step, axis=2, keepdims=True
    )
    grad_rows = grad_hidden.astype(jnp.bfloat16)
    adapter_rows = (
        ADAPTER_SCALE
        * jnp.einsum(
            "qcd,rd->qcr", grad_rows, adapter_up_weight, preferred_element_type=jnp.float32
        )
    ).astype(jnp.bfloat16)
    full_grads, full_adapter = (
        lax.all_gather(grad_rows, "tensor", axis=1, tiled=True),
        lax.all_gather(adapter_rows, "tensor", axis=1, tiled=True),
    )
    up_partial_gradient = ADAPTER_SCALE * jnp.einsum(
        "qcr,qcd->rd", adapter_input_rows, grad_rows, preferred_element_type=jnp.float32
    )
    up_share = lax.psum_scatter(
        up_partial_gradient.astype(jnp.bfloat16), "tensor", scatter_dimension=1, tiled=True
    ).astype(jnp.float32)
    adapter_back = jnp.einsum(
        "qcr,hr->qch", full_adapter, adapter_down, preferred_element_type=jnp.float32
    )
    context_wide = (
        jnp.einsum("qcd,dh->qch", full_grads, full_weight, preferred_element_type=jnp.float32)
        + adapter_back
    )
    context_grad = context_wide.astype(jnp.bfloat16)
    down_local = jnp.einsum(
        "qch,qcr->hr", context, full_adapter, preferred_element_type=jnp.float32
    )
    down_grad, up_weight_gradient = lax.psum((down_local, up_share), ("dp", "cand"))
    return (context_grad, grad_rows, down_grad, up_weight_gradient, pair_loss)


def solution(mesh):
    in_specs = (
        P("dp", "cand", "tensor"),
        P("dp", ("cand", "tensor"), None),
        P("cand", "tensor"),
        P("tensor", None),
        P(),
        P(),
        P(),
        P("dp", "cand", "tensor"),
        P("dp", "cand", "tensor"),
        P("dp"),
    )
    out_specs = (
        P("dp", "cand", "tensor"),
        P("dp", ("cand", "tensor"), None),
        P("tensor", None),
        P(None, "tensor"),
        P("dp"),
    )
    return jax.shard_map(
        on_device, mesh=mesh, in_specs=in_specs, out_specs=out_specs, check_vma=False
    )
```

profile of v0, /device:TPU:16, one launch (start us, length us, event | category | flops | bytes accessed | tf_op | source)
XLA Modules:
  0.0 1309.3 jit_solution(4041656282521602248)
XLA Ops:
  8.1 0.7 all-gather.4.cloned.1.call-update
  9.0 0.9 convolution_convert_fusion
  10.2 0.7 reshape.41
  11.0 81.7 %all-gather.4.cloned.1.call-done = bf16[3584,896]{1,0:T(8,128)(2,1)} async-done(((bf16[112,896]{1,0:T(8,128)(2,1)}), bf16[3584,896]{1,0:T(8,128)(2,1)}) %all-gather.4.cloned.1.call-update) | async-done | bytes 6422544 | tf_op jit(solution)/shard_map/all_gather | solution.py:49
  92.7 6.2 fusion.4
  99.0 0.8 reshape.42
  99.8 0.7 copy.21
  100.4 29.0 %reduce-scatter.8.cloned.1.call-done = bf16[2,32,3584]{2,1,0:T(8,128)(2,1)} async-done(((bf16[2,128,3584]{2,1,0:T(8,128)(2,1)}), bf16[2,32,3584]{2,1,0:T(8,128)(2,1)}) %reduce-scatter.8.cloned.1.call-update) | async-done | bytes 458768 | tf_op jit(solution)/shard_map/reduce_scatter | solution.py:53
  129.5 1.5 multiply_reduce_fusion.2
  131.0 0.3 multiply_reduce_fusion.1
  131.3 140.3 %all-gather = f32[128,32,2]{1,2,0:T(2,128)S(1)} all-gather(f32[1,32,2]{1,2,0:T(2,128)S(1)} %bitcast.57), channel_id=1, replica_groups=mesh['dp'=4,'cand'=32,'tensor'=4] {'cand','tensor'}, dimensions={0}, use_global_device_ids=true | all-gather | bytes 33024 | tf_op jit(solution)/shard_map/all_gather | solution.py:70
  271.8 1.2 fusion.24
  273.3 493.2 %all-reduce = (f32[2,4096]{1,0:T(2,128)S(1)}, f32[2]{0:T(128)S(1)}, f32[2]{0:T(128)S(1)}) all-reduce(f32[2,4096]{1,0:T(2,128)S(1)} %sub.29, f32[2]{0:T(128)S(1)} %get-tuple-element.6, f32[2]{0:T(128)S(1)} %get-tuple-element.5), channel_id=1, replica_groups=mesh['dp'=4,'cand'=32,'tensor'=4] {'cand','tensor'}, use_global_device_ids=true, to_apply=%region_6.7 | all-reduce | flops 8196 | bytes 65568 | tf_op jit(solution)/shard_map/psum | solution.py:78
  766.4 1.2 fusion.32
  767.7 0.3 multiply_reduce_fusion
  768.5 1.3 copy.22
  769.9 0.7 all-gather.6.cloned.1.call-update
  770.6 1.4 fusion.13
  772.1 13.7 %all_gather.15 = bf16[2,128,16]{2,0,1:T(2,128)(2,1)S(1)} all-gather(bf16[2,32,16]{2,0,1:T(2,128)(2,1)S(1)} %copy.17), channel_id=1, replica_groups=mesh['dp'=4,'cand'=32,'tensor'=4] {'tensor'}, dimensions={1}, use_global_device_ids=true | all-gather | bytes 10240 | tf_op jit(solution)/shard_map/all_gather | solution.py:95
  786.1 13.0 reduce-scatter.12.cloned.1.call-done
  799.1 1.0 copy.23
  800.1 495.1 %all-reduce.3 = (f32[896,16]{0,1:T(8,128)}, f32[16,896]{1,0:T(8,128)}) all-reduce(f32[896,16]{0,1:T(8,128)S(1)} %convolution_bitcast_fusion.1, bf16[16,896]{1,0:T(8,128)(2,1)S(1)} %copy.23), channel_id=1, replica_groups=mesh['dp'=4,'cand'=32,'tensor'=4] {'dp','cand'}, use_global_device_ids=true, to_apply=%region_10.11 | all-reduce | flops 28672 | bytes 200704 | tf_op jit(solution)/shard_map/psum | solution.py:114
  1295.2 5.5 fusion
  1300.6 1.1 fusion.12
  (49 shorter events, 2.1 us)
Async XLA Ops:
  8.0 1.0 copy-start
  8.0 84.7 %all-gather.4.cloned.1.call-start = ((), (), s32[]{:S(2)}) async-start(), calls=%async_computation.3 | async-start | bytes 6623232 | tf_op jit(solution)/shard_map/all_gather | solution.py:49
  8.7 90.2 %reduce-scatter.10.cloned.1.call-start = ((), (), s32[]{:S(2)}) async-start(), calls=%async_computation.6 | async-start | bytes 40960
  10.9 118.6 %copy-start.4 = (bf16[2,32,3584]{2,1,0:T(8,128)(2,1)S(1)}, bf16[2,32,3584]{2,1,0:T(8,128)(2,1)}, u32[]{:S(2)}) copy-start(bf16[2,32,3584]{2,1,0:T(8,128)(2,1)} %param.11) | copy-start | bytes 1376260
  10.9 118.6 %copy-start.5 = (bf16[16,3584]{1,0:T(8,128)(2,1)S(1)}, bf16[16,3584]{1,0:T(8,128)(2,1)}, u32[]{:S(2)}) copy-start(bf16[16,3584]{1,0:T(8,128)(2,1)} %param.14) | copy-start | bytes 344068
  10.9 120.1 %copy-start.6 = (f32[3584]{0:T(1024)S(1)}, f32[3584]{0:T(1024)}, u32[]{:S(2)}) copy-start(f32[3584]{0:T(1024)} %param.16) | copy-start | bytes 43012
  10.9 120.1 %copy-start.7 = (f32[3584]{0:T(1024)S(1)}, f32[3584]{0:T(1024)}, u32[]{:S(2)}) copy-start(f32[3584]{0:T(1024)} %param.15) | copy-start | bytes 43012
  10.9 260.8 %copy-start.2 = (s32[2,128,1024]{2,1,0:T(8,128)S(1)}, s32[2,128,1024]{2,1,0:T(8,128)}, u32[]{:S(2)}) copy-start(s32[2,128,1024]{2,1,0:T(8,128)} %param.18) | copy-start | bytes 3145732
  11.0 260.8 %copy-start.3 = (bf16[2,128,1024]{2,1,0:T(8,128)(2,1)S(1)}, bf16[2,128,1024]{2,1,0:T(8,128)(2,1)}, u32[]{:S(2)}) copy-start(bf16[2,128,1024]{2,1,0:T(8,128)(2,1)} %param.17) | copy-start | bytes 1572868
  11.0 118.5 %reduce-scatter.8.cloned.1.call-start = ((), (), s32[]{:S(2)}) async-start(), calls=%async_computation.4 | async-start | bytes 2293760 | tf_op jit(solution)/shard_map/reduce_scatter | solution.py:53
  98.9 700.2 %reduce-scatter.12.cloned.1.call-start = ((), (), s32[]{:S(2)}) async-start(), calls=%async_computation.7 | async-start | bytes 1146880
  130.9 637.3 %copy-start.9 = (bf16[2,32,16]{1,2,0:T(8,128)(2,1)S(1)}, bf16[2,32,16]{1,2,0:T(8,128)(2,1)}, u32[]{:S(2)}) copy-start(bf16[2,32,16]{1,2,0:T(8,128)(2,1)} %copy.21) | copy-start | bytes 6148
  768.3 1.7 copy-start.1
  769.9 525.3 %all-gather.6.cloned.1.call-start = ((), (), s32[]{:S(2)}) async-start(), calls=%async_computation.5 | async-start | bytes 2293760 | tf_op jit(solution)/shard_map/all_gather | solution.py:94
  1295.2 5.5 copy-start.8
Sparse Core Ops, SparseCore 0:
  11.2 81.4 all-gather.3
Sparse Core Ops, SparseCore 1:
  12.6 30.7 reduce-scatter.9
  99.0 30.5 reduce-scatter.7
  769.9 29.1 reduce-scatter.11
  802.0 36.1 all-gather.5
where the time goes:
time: 1310 us
  blocking collectives  1140 us (87%)
  waiting for transfers between devices  125 us (10%)
  matrix products  16.9 us (1%)
  between operations  15.9 us (1%)
    psum x1, blocking collectives, on_device(): lax.psum((down_local, up_share), ('dp', 'cand'))  495 us
    psum x1, blocking collectives, on_device(): summed_grad, loss_sum = lax.psum((score_vector, total), ('cand', 'tensor'))  493 us
    all_gather x1, blocking collectives, on_device(): all_scores = lax.all_gather(scores, ('cand', 'tensor'), axis=1, tiled=True)  140 us
    all_gather x1, waiting for transfers between devices, on_device(): full_weight = lax.all_gather(out_weight, 'cand', axis=0, tiled=True)  81.7 us
    reduce_scatter x1, waiting for transfers between devices, on_device(): lax.psum_scatter(head_terms.astype(jnp.bfloat16), 'tensor', scatter_dimen...  29 us
  transfers between devices with their start and end apart: 5, of which 3 were waited for; matrix products, arithmetic and copies ran while one was open for 1% of the time, Pallas kernels for 0%

commit v1 on v0

--- a/solution.py
+++ b/solution.py
@@ -5,6 +5,13 @@
 
 ADAPTER_SCALE = 0.5
 epsilon = 1e-06
+
+
+def all_by_exchange(x, axis, dim):
+    peers = lax.axis_size(axis)
+    parts = jnp.stack([x for _ in range(peers)])
+    parts = lax.all_to_all(parts, axis, split_axis=0, concat_axis=0)
+    return jnp.concatenate(parts, axis=dim)
 
 
 def rounded(term):
@@ -67,7 +74,7 @@
     hidden_wide = hidden_state.astype(jnp.float32)
     inv_rms = lax.rsqrt(jnp.mean(hidden_wide * hidden_wide, axis=2, keepdims=True) + epsilon)
     scores = jnp.sum(hidden_wide * inv_rms * norm_gain * score_weight, axis=2)
-    all_scores = lax.all_gather(scores, ("cand", "tensor"), axis=1, tiled=True)
+    all_scores = all_by_exchange(scores, ("cand", "tensor"), 1)
     own_start = group_index * cand_rows + tensor_index * share
     row_start = group_index * cand_rows
     col_start = tensor_index * teacher.shape[2]

time: 1310 us -> 1190 us (0.908)
  blocking collectives: 1140 us -> 998 us
  starting transfers between devices: 0.21 us -> 16.7 us
    all_gather x1 -> x0, blocking collectives: 140 us -> none  [on_device(): all_scores = lax.all_gather(scores, ('cand', 'tensor'), axis=1, tiled=True)]
    all_to_all x0 -> x1, starting transfers between devices: none -> 16.5 us  [all_by_exchange(): parts = lax.all_to_all(parts, axis, split_axis=0, concat_axis=0)]
    all_to_all x0 -> x1, waiting for transfers between devices: none -> 15.9 us  [all_by_exchange(): parts = lax.all_to_all(parts, axis, split_axis=0, concat_axis=0)]
  transfers between devices with their start and end apart: 5 -> 6, of which waited for: 3 -> 4; matrix products, arithmetic and copies ran while one was open for 1% -> 1% of each run, Pallas kernels for 0% -> 0%
where the time goes in v1:
time: 1190 us
  blocking collectives  998 us (84%)
  waiting for transfers between devices  137 us (12%)
  matrix products  16.9 us (1%)
  starting transfers between devices  16.7 us (1%)
  between operations  15.9 us (1%)
    psum x1, blocking collectives, on_device(): lax.psum((down_local, up_share), ('dp', 'cand'))  495 us
    psum x1, blocking collectives, on_device(): summed_grad, loss_sum = lax.psum((score_vector, total), ('cand', 'tensor'))  489 us
    all_gather x1, waiting for transfers between devices, on_device(): full_weight = lax.all_gather(out_weight, 'cand', axis=0, tiled=True)  81.7 us
    reduce_scatter x1, waiting for transfers between devices, on_device(): lax.psum_scatter(head_terms.astype(jnp.bfloat16), 'tensor', scatter_dimen...  29.1 us
  transfers between devices with their start and end apart: 6, of which 4 were waited for; matrix products, arithmetic and copies ran while one was open for 1% of the time, Pallas kernels for 0%

profile of v1, /device:TPU:16, one launch (start us, length us, event | category | flops | bytes accessed | tf_op | source)
XLA Modules:
  0.0 1194.3 jit_solution(7880603552292676590)
XLA Ops:
  8.1 0.7 all-gather.3.cloned.1.call-update
  9.0 0.9 convolution_convert_fusion
  10.2 0.7 reshape.49
  11.0 81.7 %all-gather.3.cloned.1.call-done = bf16[3584,896]{1,0:T(8,128)(2,1)} async-done(((bf16[112,896]{1,0:T(8,128)(2,1)}), bf16[3584,896]{1,0:T(8,128)(2,1)}) %all-gather.3.cloned.1.call-update) | async-done | bytes 6422544 | tf_op jit(solution)/shard_map/all_gather | solution.py:56
  92.7 6.2 fusion.4
  98.9 0.8 reshape.50
  99.7 0.7 copy.20
  100.4 29.1 %reduce-scatter.8.cloned.1.call-done = bf16[2,32,3584]{2,1,0:T(8,128)(2,1)} async-done(((bf16[2,128,3584]{2,1,0:T(8,128)(2,1)}), bf16[2,32,3584]{2,1,0:T(8,128)(2,1)}) %reduce-scatter.8.cloned.1.call-update) | async-done | bytes 458768 | tf_op jit(solution)/shard_map/reduce_scatter | solution.py:60
  129.5 1.4 multiply_reduce_fusion.2
  131.3 0.7 stack.2
  132.0 16.5 %all-to-all-start = ((f32[128,2,32]{2,1,0:T(2,128)}), f32[128,2,32]{2,1,0:T(2,128)S(1)}, u32[]{:S(2)}, u32[]{:S(2)}) async-start(f32[128,2,32]{2,1,0:T(2,128)} %stack.2), calls=%async_computation.1 | async-start | bytes 262144 | tf_op jit(solution)/shard_map/all_to_all | solution.py:13
  148.5 15.9 %all-to-all-done = f32[128,2,32]{2,1,0:T(2,128)S(1)} async-done(((f32[128,2,32]{2,1,0:T(2,128)}), f32[128,2,32]{2,1,0:T(2,128)S(1)}, u32[]{:S(2)}, u32[]{:S(2)}) %all-to-all-start) | async-done | bytes 32800 | tf_op jit(solution)/shard_map/all_to_all | solution.py:13
  164.7 1.2 fusion.24
  166.2 489.2 %all-reduce = (f32[2,4096]{1,0:T(2,128)S(1)}, f32[2]{0:T(128)S(1)}, f32[2]{0:T(128)S(1)}) all-reduce(f32[2,4096]{1,0:T(2,128)S(1)} %sub.29, f32[2]{0:T(128)S(1)} %get-tuple-element.6, f32[2]{0:T(128)S(1)} %get-tuple-element.5), channel_id=1, replica_groups=mesh['dp'=4,'cand'=32,'tensor'=4] {'cand','tensor'}, use_global_device_ids=true, to_apply=%region_6.7 | all-reduce | flops 8196 | bytes 65568 | tf_op jit(solution)/shard_map/psum | solution.py:85
  655.4 1.2 fusion.31
  657.5 1.3 copy.21
  658.8 0.7 all-gather.5.cloned.1.call-update
  659.5 1.4 fusion.13
  661.1 13.8 %all_gather.11 = bf16[2,128,16]{2,0,1:T(2,128)(2,1)S(1)} all-gather(bf16[2,32,16]{2,0,1:T(2,128)(2,1)S(1)} %copy.16), channel_id=1, replica_groups=mesh['dp'=4,'cand'=32,'tensor'=4] {'tensor'}, dimensions={1}, use_global_device_ids=true | all-gather | bytes 10240 | tf_op jit(solution)/shard_map/all_gather | solution.py:102
  675.1 8.9 reduce-scatter.12.cloned.1.call-done
  684.1 1.0 copy.22
  685.1 495.0 %all-reduce.3 = (f32[896,16]{0,1:T(8,128)}, f32[16,896]{1,0:T(8,128)}) all-reduce(f32[896,16]{0,1:T(8,128)S(1)} %convolution_bitcast_fusion.1, bf16[16,896]{1,0:T(8,128)(2,1)S(1)} %copy.22), channel_id=1, replica_groups=mesh['dp'=4,'cand'=32,'tensor'=4] {'dp','cand'}, use_global_device_ids=true, to_apply=%region_10.11 | all-reduce | flops 28672 | bytes 200704 | tf_op jit(solution)/shard_map/psum | solution.py:121
  1180.1 5.5 fusion
  1185.6 1.1 fusion.12
  (51 shorter events, 2.7 us)
Async XLA Ops:
  8.0 1.0 copy-start
  8.0 84.7 %all-gather.3.cloned.1.call-start = ((), (), s32[]{:S(2)}) async-start(), calls=%async_computation.4 | async-start | bytes 6623232 | tf_op jit(solution)/shard_map/all_gather | solution.py:56
  8.7 90.2 %reduce-scatter.10.cloned.1.call-start = ((), (), s32[]{:S(2)}) async-start(), calls=%async_computation.7 | async-start | bytes 40960
  10.9 118.6 %copy-start.4 = (bf16[2,32,3584]{2,1,0:T(8,128)(2,1)S(1)}, bf16[2,32,3584]{2,1,0:T(8,128)(2,1)}, u32[]{:S(2)}) copy-start(bf16[2,32,3584]{2,1,0:T(8,128)(2,1)} %param.11) | copy-start | bytes 1376260
  10.9 118.6 %copy-start.5 = (bf16[16,3584]{1,0:T(8,128)(2,1)S(1)}, bf16[16,3584]{1,0:T(8,128)(2,1)}, u32[]{:S(2)}) copy-start(bf16[16,3584]{1,0:T(8,128)(2,1)} %param.14) | copy-start | bytes 344068
  10.9 120.1 %copy-start.6 = (f32[3584]{0:T(1024)S(1)}, f32[3584]{0:T(1024)}, u32[]{:S(2)}) copy-start(f32[3584]{0:T(1024)} %param.16) | copy-start | bytes 43012
  10.9 120.1 %copy-start.7 = (f32[3584]{0:T(1024)S(1)}, f32[3584]{0:T(1024)}, u32[]{:S(2)}) copy-start(f32[3584]{0:T(1024)} %param.15) | copy-start | bytes 43012
  10.9 153.7 %copy-start.2 = (s32[2,128,1024]{2,1,0:T(8,128)S(1)}, s32[2,128,1024]{2,1,0:T(8,128)}, u32[]{:S(2)}) copy-start(s32[2,128,1024]{2,1,0:T(8,128)} %param.18) | copy-start | bytes 3145732
  11.0 153.7 %copy-start.3 = (bf16[2,128,1024]{2,1,0:T(8,128)(2,1)S(1)}, bf16[2,128,1024]{2,1,0:T(8,128)(2,1)}, u32[]{:S(2)}) copy-start(bf16[2,128,1024]{2,1,0:T(8,128)(2,1)} %param.17) | copy-start | bytes 1572868
  11.0 118.5 %reduce-scatter.8.cloned.1.call-start = ((), (), s32[]{:S(2)}) async-start(), calls=%async_computation.5 | async-start | bytes 2293760 | tf_op jit(solution)/shard_map/reduce_scatter | solution.py:60
  131.0 526.2 %copy-start.9 = (bf16[2,32,16]{1,2,0:T(8,128)(2,1)S(1)}, bf16[2,32,16]{1,2,0:T(8,128)(2,1)}, u32[]{:S(2)}) copy-start(bf16[2,32,16]{1,2,0:T(8,128)(2,1)} %copy.20) | copy-start | bytes 6148
  132.0 32.5 %all-to-all-start = ((f32[128,2,32]{2,1,0:T(2,128)}), f32[128,2,32]{2,1,0:T(2,128)S(1)}, u32[]{:S(2)}, u32[]{:S(2)}) async-start(f32[128,2,32]{2,1,0:T(2,128)} %stack.2), calls=%async_computation.1 | async-start | bytes 262144 | tf_op jit(solution)/shard_map/all_to_all | solution.py:13
  148.5 535.6 %reduce-scatter.12.cloned.1.call-start = ((), (), s32[]{:S(2)}) async-start(), calls=%async_computation.8 | async-start | bytes 1146880
  657.2 1.7 copy-start.1
  658.8 521.3 %all-gather.5.cloned.1.call-start = ((), (), s32[]{:S(2)}) async-start(), calls=%async_computation.6 | async-start | bytes 2293760 | tf_op jit(solution)/shard_map/all_gather | solution.py:101
  1180.1 5.5 copy-start.8
Sparse Core Ops, SparseCore 0:
  11.2 81.4 all-gather.2
Sparse Core Ops, SparseCore 1:
  12.6 30.7 reduce-scatter.9
  99.0 30.5 reduce-scatter.7
  658.9 25.1 reduce-scatter.11
  687.0 36.0 all-gather.4
